TPU v7x, 256 devices: a whole 4x4x8 slice. The times are simulated.
256 devices in a mesh: wide: 64 (over z_lo, x, y), narrow: 4 (over z_hi, core).
Axes of the slice: x: 4, y: 4, z: 8 (z_hi: 2, z_lo: 4; z = z_hi * 4 + z_lo), core: 2. Of those that a mesh axis runs over, the one named last changes fastest.
Arguments:
- constraint_mats: bfloat16 [1024, 256, 256], P(('narrow', 'wide')), may hold values from -0.375 to 0.375
- primal_matrix: bfloat16 [256, 256], replicated, may hold values from -0.25 to 0.25
- inverse_dual_iterate: bfloat16 [256, 256], replicated, may hold values from -0.25 to 0.25
Outputs:
- schur: float32 [1024, 1024], P(('narrow', 'wide'))
All inputs are finite; a program needn't handle non-finite values.
Results may differ from a plain program's by a relative error of at most 0.0029.
Values may be sent and summed in bfloat16 or wider, within the bound.
A program may use at most 64 MiB of HBM per device.

v0:
```python
import jax
import jax.numpy as jnp
from jax import lax
from jax.sharding import PartitionSpec as P


def contract(u_rows, constraint_row_stack):
    return lax.dot_general(
        u_rows, constraint_row_stack, (((1,), (1,)), ((), ())), preferred_element_type=jnp.float32
    )


def body(constraint_mats, primal_matrix, inverse_dual_iterate):
    count = constraint_mats.shape[0]
    order = constraint_mats.shape[1]
    left_product = jnp.einsum(
        "ab,ibc->iac", primal_matrix, constraint_mats, preferred_element_type=jnp.float32
    ).astype(jnp.bfloat16)
    product_matrices = jnp.einsum(
        "lsx,xm->lsm", left_product, inverse_dual_iterate, preferred_element_type=jnp.float32
    ).astype(jnp.bfloat16)
    u_flat = product_matrices.reshape(count, order * order)
    a_flat = constraint_mats.reshape(count, order * order)
    product_pieces, a_slices = (
        lax.all_to_all(u_flat, "wide", split_axis=1, concat_axis=0, tiled=True),
        lax.all_to_all(a_flat, "wide", split_axis=1, concat_axis=0, tiled=True),
    )
    u_every, a_every = (
        lax.all_gather(product_pieces, "narrow", axis=0, tiled=True),
        lax.all_gather(a_slices, "narrow", axis=0, tiled=True),
    )
    partial_value = 0.5 * (contract(product_pieces, a_every) + contract(a_slices, u_every))
    schur = lax.psum_scatter(partial_value, "wide", scatter_dimension=0, tiled=True)
    return schur


def solution(mesh):
    in_specs = (P(("narrow", "wide"), None, None), P(), P())
    out_specs = P(("narrow", "wide"), None)
    return jax.shard_map(body, mesh=mesh, in_specs=in_specs, out_specs=out_specs, check_vma=False)
```

profile of v0, /device:TPU:8, one launch (start us, length us, event | category | flops | bytes accessed | tf_op | source)
XLA Modules:
  0.0 844.7 jit_solution(17084348686302862161)
XLA Ops:
  6.5 1.4 all_to_all.32
  7.9 0.0 copy-start.2
  7.9 0.0 copy-start.3
  8.0 0.4 copy.11
  8.4 28.8 %all_to_all.38 = bf16[4,64,1024]{2,0,1:T(4,128)(2,1)S(1)} all-to-all(bf16[4,64,1024]{2,0,1:T(4,128)(2,1)S(1)} %copy.11), channel_id=1, replica_groups=mesh['wide'=64,'narrow'=4] {'wide'}, dimensions={1} | all-to-all | bytes 1048576 | tf_op jit(solution)/shard_map/all_to_all | solution.py:26
  37.2 0.9 all_to_all.35
  38.1 0.0 all-gather.3.cloned.1.call-update
  38.1 0.0 all-gather.5.cloned.1.call-start
  38.2 0.8 convolution_convert_fusion
  39.0 0.3 all_to_all.28
  39.3 0.4 copy.10
  39.8 44.4 %all_to_all.39 = bf16[4,64,1024]{2,0,1:T(4,128)(2,1)S(1)} all-to-all(bf16[4,64,1024]{2,0,1:T(4,128)(2,1)S(1)} %copy.10), channel_id=1, replica_groups=mesh['wide'=64,'narrow'=4] {'wide'}, dimensions={1} | all-to-all | bytes 1048576 | tf_op jit(solution)/shard_map/all_to_all | solution.py:25
  84.2 0.9 all_to_all.31
  85.1 0.0 all-gather.5.cloned.1.call-update
  85.1 0.0 all-reduce.3.cloned.1.call-start
  85.2 0.0 all-gather.3.cloned.1.call-done
  85.2 2.5 fusion.6
  87.7 0.0 copy-start.4
  87.8 38.3 %all-gather.5.cloned.1.call-done = bf16[1024,1024]{1,0:T(8,128)(2,1)} async-done(((bf16[256,1024]{1,0:T(8,128)(2,1)}), bf16[1024,1024]{1,0:T(8,128)(2,1)}) %all-gather.5.cloned.1.call-update) | async-done | bytes 2097168 | tf_op jit(solution)/shard_map/all_gather | solution.py:29
  126.0 3.3 fusion.1
  129.3 0.0 all-reduce.3.cloned.1.call-update
  129.4 0.6 dynamic-slice
  130.6 706.2 %all-reduce.3.cloned.1.call-done = f32[256,1024]{1,0:T(8,128)} async-done(((f32[256,1024]{1,0:T(8,128)}), f32[256,1024]{1,0:T(8,128)}) %all-reduce.3.cloned.1.call-update) | async-done | bytes 1048592
  836.8 1.4 constant_dynamic-slice_fusion
  (8 shorter events, 0.0 us)
Async XLA Ops:
  6.5 31.7 %copy-start = (bf16[256,256]{1,0:T(8,128)(2,1)S(1)}, bf16[256,256]{1,0:T(8,128)(2,1)}, u32[]{:S(2)}) copy-start(bf16[256,256]{1,0:T(8,128)(2,1)} %param.5) | copy-start | bytes 393220
  6.5 78.6 %all-gather.3.cloned.1.call-start = ((), (), s32[]{:S(2)}) async-start(), calls=%async_computation.2 | async-start | bytes 2621440 | tf_op jit(solution)/shard_map/all_gather | solution.py:30
  7.9 30.3 %copy-start.2 = (bf16[4,256,256]{2,1,0:T(8,128)(2,1)S(1)}, bf16[4,256,256]{2,1,0:T(8,128)(2,1)}, u32[]{:S(2)}) copy-start(bf16[4,256,256]{2,1,0:T(8,128)(2,1)} %param.3) | copy-start | bytes 1572868
  7.9 30.3 %copy-start.3 = (bf16[256,256]{1,0:T(8,128)(2,1)S(1)}, bf16[256,256]{1,0:T(8,128)(2,1)}, u32[]{:S(2)}) copy-start(bf16[256,256]{1,0:T(8,128)(2,1)} %param.4) | copy-start | bytes 393220
  38.1 87.9 %all-gather.5.cloned.1.call-start = ((), (), s32[]{:S(2)}) async-start(), calls=%async_computation.3 | async-start | bytes 2621440 | tf_op jit(solution)/shard_map/all_gather | solution.py:29
  85.1 40.9 %copy-start.1 = (bf16[256,1024]{1,0:T(8,128)(2,1)S(1)}, bf16[256,1024]{1,0:T(8,128)(2,1)}, u32[]{:S(2)}) copy-start(bf16[256,1024]{1,0:T(8,128)(2,1)} %all_to_all.35) | copy-start | bytes 1572868
  85.1 751.7 %all-reduce.3.cloned.1.call-start = ((), (), s32[]{:S(2)}) async-start(), calls=%async_computation.4 | async-start | bytes 2097152
  87.7 41.6 %copy-start.4 = (u32[256]{0:T(256)S(1)}, u32[256]{0:T(256)}, u32[]{:S(2)}) copy-start(u32[256]{0:T(256)} %constant.5) | copy-start | bytes 3076
Sparse Core Ops, SparseCore 0:
  38.3 42.0 all-gather.2
  85.2 40.7 all-gather.4
  129.5 707.3 all-reduce.2
where the time goes:
time: 845 us
  waiting for transfers between devices  745 us (88%)
  blocking collectives  73.2 us (9%)
  between operations  13.9 us (2%)
    unnamed x4, waiting for transfers between devices  706 us
    all_to_all x1, blocking collectives, body(): lax.all_to_all(u_flat, 'wide', split_axis=1, concat_axis=0, tiled=True)  44.4 us
    all_gather x1, waiting for transfers between devices, body(): lax.all_gather(product_pieces, 'narrow', axis=0, tiled=True)  38.3 us
    all_to_all x1, blocking collectives, body(): lax.all_to_all(a_flat, 'wide', split_axis=1, concat_axis=0, tiled=True)  28.8 us
  transfers between devices with their start and end apart: 3, of which 2 were waited for; matrix products, arithmetic and copies ran while one was open for 1% of the time, Pallas kernels for 0%

commit v1 on v0

v1 whole, which is shorter than its diff:
```python
import jax
import jax.numpy as jnp
from jax import lax
from jax.sharding import PartitionSpec as P


def contract(u_rows, constraint_row_stack):
    return lax.dot_general(
        u_rows, constraint_row_stack, (((1,), (1,)), ((), ())), preferred_element_type=jnp.float32
    )


def body(constraint_mats, primal_matrix, inverse_dual_iterate):
    count = constraint_mats.shape[0]
    order = constraint_mats.shape[1]
    wide = lax.axis_size("wide")
    left_product = jnp.einsum(
        "ab,ibc->iac", primal_matrix, constraint_mats, preferred_element_type=jnp.float32
    ).astype(jnp.bfloat16)
    product_matrices = jnp.einsum(
        "lsx,xm->lsm", left_product, inverse_dual_iterate, preferred_element_type=jnp.float32
    ).astype(jnp.bfloat16)
    u_flat = product_matrices.reshape(count, order * order)
    a_flat = constraint_mats.reshape(count, order * order)
    both = jnp.stack([u_flat, a_flat])
    pieces = lax.all_to_all(both, "wide", split_axis=2, concat_axis=1, tiled=True)
    every = lax.all_gather(pieces, "narrow", axis=1, tiled=True)
    partial_value = 0.5 * (contract(pieces[0], every[1]) + contract(pieces[1], every[0]))
    rows = partial_value.shape[0] // wide
    blocks = partial_value.reshape(wide, rows, partial_value.shape[1])
    arrived = lax.all_to_all(blocks, "wide", split_axis=0, concat_axis=0, tiled=True)
    return jnp.sum(arrived, axis=0)


def solution(mesh):
    in_specs = (P(("narrow", "wide"), None, None), P(), P())
    out_specs = P(("narrow", "wide"), None)
    return jax.shard_map(body, mesh=mesh, in_specs=in_specs, out_specs=out_specs, check_vma=False)
```

time: 845 us -> 424 us (0.50)
  waiting for transfers between devices: 745 us -> 63.5 us
  local copies, waits for them, and re-layouts: 6.34 us -> 265 us
    unnamed x4 -> x1, waiting for transfers between devices: 706 us -> 0.02 us
    unnamed x12 -> x6, local copies, waits for them, and re-layouts: 1.98 us -> 134 us
    all_to_all x6 -> x2, local copies, waits for them, and re-layouts: 4.36 us -> 67.4 us  [body(): lax.all_to_all(both, 'wide', split_axis=2, concat_axis=1, tiled=True)]
    another operation x0 -> x3, local copies, waits for them, and re-layouts: none -> 52.9 us  [body(): both = jnp.stack([u_flat, a_flat])]
    all_gather x2 -> x1, waiting for transfers between devices: 38.3 us -> 63.5 us  [body(): every = lax.all_gather(pieces, 'narrow', axis=1, tiled=True)]
    slice x0 -> x2, local copies, waits for them, and re-layouts: none -> 9.25 us  [the longest x1 8.88 us: body(): every[1]]
  transfers between devices with their start and end apart: 3 -> 1, of which waited for: 2 -> 1; matrix products, arithmetic and copies ran while one was open for 1% -> 0% of each run, Pallas kernels for 0% -> 0%
where the time goes in v1:
time: 424 us; the launch traced here: 423 us
  local copies, waits for them, and re-layouts  265 us (62%)
  blocking collectives  75.8 us (18%)
  waiting for transfers between devices  63.5 us (15%)
  between operations  13.5 us (3%)
    unnamed x6, local copies, waits for them, and re-layouts  134 us
    all_to_all x2, local copies, waits for them, and re-layouts, body(): lax.all_to_all(both, 'wide', split_axis=2, concat_axis=1, tiled=True)  67.4 us
    all_gather x1, waiting for transfers between devices, body(): every = lax.all_gather(pieces, 'narrow', axis=1, tiled=True)  63.5 us
    another operation x3, local copies, waits for them, and re-layouts, body(): both = jnp.stack([u_flat, a_flat])  52.9 us
    all_to_all x1, blocking collectives, body(): lax.all_to_all(both, 'wide', split_axis=2, concat_axis=1, tiled=True)  39.8 us
    all_to_all x1, blocking collectives, body(): lax.all_to_all(blocks, 'wide', split_axis=0, concat_axis=0, tiled=True)  36 us
    slice x1, local copies, waits for them, and re-layouts, body(): every[1]  8.88 us
  transfers between devices with their start and end apart: 1, of which 1 were waited for; matrix products, arithmetic and copies ran while one was open for 0% of the time, Pallas kernels for 0%

profile of v1, /device:TPU:8, one launch (start us, length us, event | category | flops | bytes accessed | tf_op | source)
XLA Modules:
  0.0 422.6 jit_solution(4422344716620643686)
XLA Ops:
  6.5 0.0 copy-start
  6.5 0.0 all-gather.2.cloned.1.call-start
  6.5 1.5 stack_reshape.7
  8.0 1.8 convolution_convert_fusion
  9.9 0.4 stack_reshape.6
  10.3 0.7 pad_maximum_fusion
  11.0 51.0 %copy.18 = bf16[2,4,65536]{1,0,2:T(2,128)(2,1)} copy(bf16[2,4,65536]{2,1,0:T(4,128)(2,1)S(1)} %pad_maximum_fusion) | data formatting | bytes 2097152 | tf_op jit(solution)/shard_map/stack | solution.py:25
  62.0 61.1 %reshape.10 = bf16[64,2,4096]{2,1,0:T(2,128)(2,1)S(1)} reshape(bf16[65536,2,4]{2,1,0:T(2,128)(2,1)} %bitcast.29) | data formatting | bytes 2097152
  123.2 39.8 %all_to_all.23 = bf16[64,2,4096]{2,1,0:T(2,128)(2,1)S(1)} all-to-all(bf16[64,2,4096]{2,1,0:T(2,128)(2,1)S(1)} %reshape.10), channel_id=1, replica_groups=mesh['wide'=64,'narrow'=4] {'wide'}, dimensions={0} | all-to-all | bytes 2097152 | tf_op jit(solution)/shard_map/all_to_all | solution.py:26
  163.0 73.3 %reshape.11 = bf16[65536,2,4]{2,1,0:T(2,128)(2,1)} reshape(bf16[64,2,4096]{2,1,0:T(2,128)(2,1)S(1)} %all_to_all.23) | data formatting | bytes 2097152
  236.3 65.3 %copy.19 = bf16[2,4,64,1024]{3,1,2,0:T(4,128)(2,1)S(1)} copy(bf16[2,4,64,1024]{1,0,3,2:T(2,128)(2,1)} %bitcast.30) | data formatting | bytes 2097152 | tf_op jit(solution)/shard_map/all_to_all | solution.py:26
  301.6 2.1 copy.20
  303.7 0.0 all-gather.2.cloned.1.call-update
  303.7 0.4 fusion.9
  304.1 0.1 squeeze.12
  304.2 0.1 squeeze.14
  304.3 63.5 %all-gather.2.cloned.1.call-done = bf16[2,1024,1024]{2,0,1:T(2,128)(2,1)} async-done(((bf16[2,256,1024]{2,0,1:T(2,128)(2,1)}), bf16[2,1024,1024]{2,0,1:T(2,128)(2,1)}) %all-gather.2.cloned.1.call-update) | async-done | bytes 4194320 | tf_op jit(solution)/shard_map/all_gather | solution.py:27
  367.8 8.9 %fusion.8 = (bf16[1,1024,1024]{2,0,1:T(2,128)(2,1)S(1)}, bf16[1,1024,1024]{2,0,1:T(2,128)(2,1)S(1)}) fusion(bf16[2,1024,1024]{2,0,1:T(2,128)(2,1)} %all-gather.2.cloned.1.call-done), kind=kLoop, calls=%fused_computation.12 | loop fusion | bytes 8388608 | tf_op jit(solution)/shard_map/slice | solution.py:28
  376.7 0.9 fusion
  377.6 0.0 copy-start.1
  377.6 1.0 fusion.3
  378.6 0.3 reshape.7
  378.9 36.0 %all_to_all.24 = f32[64,4,1024]{2,1,0:T(4,128)S(1)} all-to-all(f32[64,4,1024]{2,1,0:T(4,128)S(1)} %reshape.7), channel_id=1, replica_groups=mesh['wide'=64,'narrow'=4] {'wide'}, dimensions={0} | all-to-all | bytes 2097152 | tf_op jit(solution)/shard_map/all_to_all | solution.py:31
  414.9 0.8 reduce_sum.9
  (2 shorter events, 0.0 us)
Async XLA Ops:
  6.5 1.5 copy-start
  6.5 361.3 %all-gather.2.cloned.1.call-start = ((), (), s32[]{:S(2)}) async-start(), calls=%async_computation.2 | async-start | bytes 5242880 | tf_op jit(solution)/shard_map/all_gather | solution.py:27
  377.6 38.1 %copy-start.1 = (bf16[256,256]{1,0:T(8,128)(2,1)S(1)}, bf16[256,256]{1,0:T(8,128)(2,1)}, u32[]{:S(2)}) copy-start(bf16[256,256]{1,0:T(8,128)(2,1)} %param.5) | copy-start | bytes 393220
Sparse Core Ops, SparseCore 0:
  303.8 63.9 all-gather.1
